TPU v7x, 768 devices: a whole 4x8x12 slice. The times are simulated.
768 devices in a mesh: seq: 16 (over y, core), head: 12 (over x, z_hi), rep: 4 (over z_lo).
Axes of the slice: x: 4, y: 8, z: 12 (z_hi: 3, z_lo: 4; z = z_hi * 4 + z_lo), core: 2. Of those that a mesh axis runs over, the one named last changes fastest.
Arguments:
- queries: bfloat16 [16384, 3072], P(('seq', 'rep'), 'head'), may hold values from -190 to 190
- keys: bfloat16 [16384, 3072], P(('seq', 'rep'), 'head'), may hold values from -6 to 6
- values: bfloat16 [16384, 3072], P(('seq', 'rep'), 'head'), may hold values from -6 to 6
- grad_output: bfloat16 [16384, 3072], P(('seq', 'rep'), 'head'), may hold values from -12 to 12
- out_weight: bfloat16 [3072, 3072], P('head'), may hold values from -0.109375 to 0.109375
- text_keys: bfloat16 [256, 3072], P(None, 'head'), may hold values from -7 to 7
- text_values: bfloat16 [256, 3072], P(None, 'head'), may hold values from -6 to 6
- mask_lists: int32 [128, 3], replicated, may hold values from 0 to 127, as said below
- text_owner: int32 [256], replicated, may hold values from 0 to 63, as said below
Outputs:
- query_grads: bfloat16 [16384, 3072], P(('seq', 'rep'), 'head')
- key_grads: bfloat16 [16384, 3072], P(('seq', 'rep'), 'head')
- value_grads: bfloat16 [16384, 3072], P(('seq', 'rep'), 'head')
- text_key_grads: bfloat16 [512, 3072], P(('seq', 'rep'), 'head')
- text_value_grads: bfloat16 [512, 3072], P(('seq', 'rep'), 'head')
Inputs may be any that keep to these rules, and one draw needn't show every extreme that they name: Video tokens s * 256 to (s + 1) * 256 - 1 form slab s. Row t of mask_lists begins with t itself; its other 2 entries are distinct existing tiles other than t of the slabs t // 2 - 1, t // 2 and t // 2 + 1. `text_owner`: no slab owns more than 8 text tokens, and some slab owns exactly 8.
All inputs are finite; a program needn't handle non-finite values.
Results may differ from a plain program's by a relative error of at most 0.0156.
Values may be sent and summed in bfloat16 or wider, within the bound.
A program may use at most 32 MiB of HBM per device.

v0:
```python
import jax
import jax.numpy as jnp
from jax import lax
from jax.sharding import PartitionSpec as P

HD = 128
TILE = 128


def extended(cells, sides, width):
    for axis, dim in sides:
        count = lax.axis_size(axis)
        ends = count - 1
        head = lax.slice_in_dim(cells, 0, width, axis=dim)
        tail = lax.slice_in_dim(cells, cells.shape[dim] - width, cells.shape[dim], axis=dim)
        cells = jnp.concatenate(
            [
                lax.ppermute(tail, axis, [(i, (i + 1) % count) for i in range(ends)]),
                cells,
                lax.ppermute(head, axis, [((i + 1) % count, i) for i in range(ends)]),
            ],
            axis=dim,
        )
    return cells


def tile_allowed(lists, first_tile, count):
    tile_ids = first_tile + jnp.arange(count, dtype=jnp.int32)
    return jnp.any(lists[:, :, None] == tile_ids[None, None, :], axis=1)


def token_mask(allowed):
    return jnp.repeat(jnp.repeat(allowed, TILE, axis=0), TILE, axis=1)


def local(
    queries, keys, values, grad_output, out_weight, text_keys, text_values, mask_lists, text_owner
):
    frame = queries.shape[0]
    width = queries.shape[1]
    heads_here = width // HD
    tiles_here = frame // TILE
    text_count = text_keys.shape[0]
    scale = HD ** (-0.5)
    slab = lax.axis_index(("seq", "rep"))
    grad_sum = lax.dot_general(
        lax.all_gather(grad_output, "head", axis=1, tiled=True),
        out_weight,
        (((1,), (1,)), ((), ())),
        preferred_element_type=jnp.float32,
    )
    grad_heads = grad_sum.astype(jnp.bfloat16)
    wide = extended(jnp.stack([keys, values]), ((("seq", "rep"), 1),), frame)
    own_lists = lax.dynamic_slice_in_dim(mask_lists, slab * tiles_here, tiles_here, 0)
    video_mask = token_mask(tile_allowed(own_lists, (slab - 1) * tiles_here, 3 * tiles_here))
    q_rows = queries.reshape(frame, heads_here, HD)
    g_rows = grad_heads.reshape(frame, heads_here, HD)
    near_keys = wide[0].reshape(3 * frame, heads_here, HD)
    near_values = wide[1].reshape(3 * frame, heads_here, HD)
    text_k = text_keys.reshape(text_count, heads_here, HD)
    text_v = text_values.reshape(text_count, heads_here, HD)
    video_scores = scale * jnp.einsum(
        "qhe,khe->hqk", q_rows, near_keys, preferred_element_type=jnp.float32
    )
    video_scores = jnp.where(video_mask[None], video_scores, -jnp.inf)
    text_scores = scale * jnp.einsum(
        "qhe,khe->hqk", q_rows, text_k, preferred_element_type=jnp.float32
    )
    top = jnp.maximum(jnp.max(video_scores, axis=2), jnp.max(text_scores, axis=2))
    total = jnp.sum(jnp.exp(video_scores - top[:, :, None]), axis=2) + jnp.sum(
        jnp.exp(text_scores - top[:, :, None]), axis=2
    )
    lse = top + jnp.log(total)
    video_prob = jnp.exp(video_scores - lse[:, :, None])
    text_prob = jnp.exp(text_scores - lse[:, :, None])
    video_half = video_prob.astype(jnp.bfloat16)
    text_half = text_prob.astype(jnp.bfloat16)
    attended = jnp.einsum(
        "hqk,khe->qhe", video_half, near_values, preferred_element_type=jnp.float32
    )
    attended = attended + jnp.einsum(
        "hqk,khe->qhe", text_half, text_v, preferred_element_type=jnp.float32
    )
    delta = jnp.einsum("qhe,qhe->hq", g_rows.astype(jnp.float32), attended)
    video_dprob = jnp.einsum(
        "qhe,khe->hqk", g_rows, near_values, preferred_element_type=jnp.float32
    )
    text_dprob = jnp.einsum("qhe,khe->hqk", g_rows, text_v, preferred_element_type=jnp.float32)
    video_ds = (video_prob * (video_dprob - delta[:, :, None])).astype(jnp.bfloat16)
    text_ds = (text_prob * (text_dprob - delta[:, :, None])).astype(jnp.bfloat16)
    query_sum = jnp.einsum("hqk,khe->qhe", video_ds, near_keys, preferred_element_type=jnp.float32)
    query_sum = query_sum + jnp.einsum(
        "hqk,khe->qhe", text_ds, text_k, preferred_element_type=jnp.float32
    )
    query_grads = (scale * query_sum).reshape(frame, width).astype(jnp.bfloat16)
    key_wide = scale * jnp.einsum(
        "hqk,qhe->khe", video_ds, q_rows, preferred_element_type=jnp.float32
    )
    value_wide = jnp.einsum("hqk,qhe->khe", video_half, g_rows, preferred_element_type=jnp.float32)
    grads_wide = jnp.stack(
        [key_wide.reshape(3 * frame, width), value_wide.reshape(3 * frame, width)]
    )
    outgoing = jnp.concatenate([grads_wide[:, :frame], grads_wide[:, 2 * frame :]], axis=1)
    arrived = extended(outgoing.astype(jnp.bfloat16), ((("seq", "rep"), 1),), frame).astype(
        outgoing.dtype
    )
    own_grads = grads_wide[:, frame : 2 * frame] + arrived[:, :frame] + arrived[:, 3 * frame :]
    key_grads = own_grads[0].astype(jnp.bfloat16)
    value_grads = own_grads[1].astype(jnp.bfloat16)
    text_key_part = (
        scale * jnp.einsum("hqk,qhe->khe", text_ds, q_rows, preferred_element_type=jnp.float32)
    ).reshape(text_count, width)
    text_value_part = jnp.einsum(
        "hqk,qhe->khe", text_half, g_rows, preferred_element_type=jnp.float32
    ).reshape(text_count, width)
    groups = lax.axis_size(("seq", "rep"))
    capacity = 2 * text_count // groups
    owner_hot = (text_owner[:, None] == jnp.arange(groups, dtype=jnp.int32)[None, :]).astype(
        jnp.int32
    )
    rank = jnp.sum(owner_hot * (jnp.cumsum(owner_hot, axis=0) - 1), axis=1)
    slot = text_owner * capacity + rank
    placing = (jnp.arange(groups * capacity, dtype=jnp.int32)[:, None] == slot[None, :]).astype(
        jnp.float32
    )
    key_slots = jnp.dot(
        placing, text_key_part, precision=lax.Precision.HIGHEST, preferred_element_type=jnp.float32
    )
    value_slots = jnp.dot(
        placing,
        text_value_part,
        precision=lax.Precision.HIGHEST,
        preferred_element_type=jnp.float32,
    )
    key_mine, value_mine = (
        lax.psum_scatter(key_slots, ("seq", "rep"), scatter_dimension=0, tiled=True),
        lax.psum_scatter(value_slots, ("seq", "rep"), scatter_dimension=0, tiled=True),
    )
    return (
        query_grads,
        key_grads,
        value_grads,
        key_mine.astype(jnp.bfloat16),
        value_mine.astype(jnp.bfloat16),
    )


def solution(mesh):
    return jax.shard_map(
        local,
        mesh=mesh,
        in_specs=(
            P(("seq", "rep"), "head"),
            P(("seq", "rep"), "head"),
            P(("seq", "rep"), "head"),
            P(("seq", "rep"), "head"),
            P("head", None),
            P(None, "head"),
            P(None, "head"),
            P(),
            P(),
        ),
        out_specs=(
            P(("seq", "rep"), "head"),
            P(("seq", "rep"), "head"),
            P(("seq", "rep"), "head"),
            P(("seq", "rep"), "head"),
            P(("seq", "rep"), "head"),
        ),
        check_vma=False,
    )
```

profile of v0, /device:TPU:1, one launch (start us, length us, event | category | flops | bytes accessed | tf_op | source)
XLA Modules:
  0.0 681.2 jit_solution(16555483265407708650)
XLA Ops:
  7.2 1.1 copy.62
  9.4 9.0 %collective-permute-start.1 = (bf16[2,256,256]{1,2,0:T(8,128)(2,1)S(1)}, bf16[2,256,256]{1,2,0:T(8,128)(2,1)S(1)}, u32[]{:S(2)}, u32[]{:S(2)}) collective-permute-start(bf16[2,256,256]{1,2,0:T(8,128)(2,1)S(1)} %pad_maximum_fusion.5), channel_id=1, source_target_pairs={{1,0},{2,1},{3,2},{48,3},{49,48},{50,49},{51,50},{96,51},{97,96},{... | collective-permute-start | bytes 786440 | tf_op jit(solution)/shard_map/ppermute | solution.py:20
  18.4 1.9 collective-permute-start
  25.0 5.8 collective-permute-done
  33.7 77.5 %all-gather.2.cloned.1.call-done = bf16[256,3072]{1,0:T(8,128)(2,1)} async-done(((bf16[256,256]{1,0:T(8,128)(2,1)}), bf16[256,3072]{1,0:T(8,128)(2,1)}) %all-gather.2.cloned.1.call-update) | async-done | bytes 1572880 | tf_op jit(solution)/shard_map/all_gather | solution.py:47
  111.2 2.1 convolution_convert_fusion
  114.0 1.2 fusion.15
  115.3 1.5 fusion.10
  116.7 1.4 multiply_convert_fusion
  119.1 1.3 convolution_multiply_fusion
  120.3 2.3 copy.85
  122.7 1.3 fusion.20
  124.0 2.4 copy.86
  126.8 1.2 fusion.16
  129.1 1.9 collective-permute-start.2
  131.0 5.4 collective-permute-start.3
  137.6 1.7 copy.91
  139.3 3.1 collective-permute-done.2
  142.4 4.9 collective-permute-done.3
  147.3 1.1 fusion.14
  149.1 238.7 %reduce-scatter.5.cloned.1.call-done = f32[8,256]{1,0:T(8,128)} async-done(((f32[512,256]{1,0:T(8,128)}), f32[8,256]{1,0:T(8,128)}) %reduce-scatter.5.cloned.1.call-update) | async-done | bytes 8208 | tf_op jit(solution)/shard_map/reduce_scatter | solution.py:137
  387.9 1.3 convert_element_type.58
  389.2 284.2 %reduce-scatter.3.cloned.1.call-done = f32[8,256]{1,0:T(8,128)} async-done(((f32[512,256]{1,0:T(8,128)}), f32[8,256]{1,0:T(8,128)}) %reduce-scatter.3.cloned.1.call-update) | async-done | bytes 8208 | tf_op jit(solution)/shard_map/reduce_scatter | solution.py:136
  673.4 1.3 convert_element_type.57
  (85 shorter events, 13.3 us)
Async XLA Ops:
  7.2 104.1 %copy-start = (bf16[256,3072]{1,0:T(8,128)(2,1)S(1)}, bf16[256,3072]{1,0:T(8,128)(2,1)}, u32[]{:S(2)}) copy-start(bf16[256,3072]{1,0:T(8,128)(2,1)} %param.13) | copy-start | bytes 4718596
  7.2 17.3 %copy-start.20 = (bf16[256,256]{1,0:T(8,128)(2,1)S(1)}, bf16[256,256]{1,0:T(8,128)(2,1)}, u32[]{:S(2)}) copy-start(bf16[256,256]{1,0:T(8,128)(2,1)} %param.9) | copy-start | bytes 393220
  7.2 17.4 %copy-start.21 = (bf16[256,256]{1,0:T(8,128)(2,1)S(1)}, bf16[256,256]{1,0:T(8,128)(2,1)}, u32[]{:S(2)}) copy-start(bf16[256,256]{1,0:T(8,128)(2,1)} %param.14) | copy-start | bytes 393220
  7.2 104.0 %all-gather.2.cloned.1.call-start = ((), (), s32[]{:S(2)}) async-start(), calls=%async_computation.2 | async-start | bytes 1703936 | tf_op jit(solution)/shard_map/all_gather | solution.py:47
  9.4 15.6 %collective-permute-start.1 = (bf16[2,256,256]{1,2,0:T(8,128)(2,1)S(1)}, bf16[2,256,256]{1,2,0:T(8,128)(2,1)S(1)}, u32[]{:S(2)}, u32[]{:S(2)}) collective-permute-start(bf16[2,256,256]{1,2,0:T(8,128)(2,1)S(1)} %pad_maximum_fusion.5), channel_id=1, source_target_pairs={{1,0},{2,1},{3,2},{48,3},{49,48},{50,49},{51,50},{96,51},{97,96},{... | collective-permute-start | bytes 786440 | tf_op jit(solution)/shard_map/ppermute | solution.py:20
  18.4 12.4 %collective-permute-start = (bf16[2,256,256]{1,2,0:T(8,128)(2,1)S(1)}, bf16[2,256,256]{1,2,0:T(8,128)(2,1)S(1)}, u32[]{:S(2)}, u32[]{:S(2)}) collective-permute-start(bf16[2,256,256]{1,2,0:T(8,128)(2,1)S(1)} %pad_maximum_fusion.5), channel_id=1, source_target_pairs={{0,1},{1,2},{2,3},{3,48},{48,49},{49,50},{50,51},{51,96},{96,97},{... | collective-permute-start | bytes 786440 | tf_op jit(solution)/shard_map/ppermute | solution.py:18
  20.4 367.5 %reduce-scatter.5.cloned.1.call-start = ((), (), s32[]{:S(2)}) async-start(), calls=%async_computation.4 | async-start | bytes 532480 | tf_op jit(solution)/shard_map/reduce_scatter | solution.py:137
  24.6 6.2 copy-start.13
  24.7 6.2 copy-start.17
  25.0 7.2 %copy-start.1 = (f32[2,256,256]{1,2,0:T(8,128)}, f32[2,256,256]{1,2,0:T(8,128)S(1)}, u32[]{:S(2)}) copy-start(f32[2,256,256]{1,2,0:T(8,128)S(1)} %get-tuple-element.29) | copy-start | bytes 1572868
  111.2 2.1 copy-start.2
  115.2 558.2 %reduce-scatter.3.cloned.1.call-start = ((), (), s32[]{:S(2)}) async-start(), calls=%async_computation.3 | async-start | bytes 532480 | tf_op jit(solution)/shard_map/reduce_scatter | solution.py:136
  116.7 2.3 copy-start.15
  119.1 3.6 copy-start.11
  123.9 2.4 copy-start.3
  123.9 2.4 copy-start.12
  124.0 2.4 copy-start.19
  124.0 2.6 copy-start.16
  126.4 1.7 copy-start.4
  128.1 8.4 %copy-start.7 = (bf16[2,256,768]{1,2,0:T(8,128)(2,1)S(1)}, bf16[2,256,768]{1,2,0:T(8,128)(2,1)}, u32[]{:S(2)}) copy-start(bf16[2,256,768]{1,2,0:T(8,128)(2,1)} %copy-done.6) | copy-start | bytes 2359300
  128.1 8.4 %copy-start.9 = (bf16[1,768,256]{1,2,0:T(8,128)(2,1)S(1)}, bf16[1,768,256]{1,2,0:T(8,128)(2,1)}, u32[]{:S(2)}) copy-start(bf16[1,768,256]{1,2,0:T(8,128)(2,1)} %copy-done.8) | copy-start | bytes 1179652
  128.2 8.5 %copy-start.18 = (bf16[256,256]{0,1:T(8,128)(2,1)S(1)}, bf16[256,256]{0,1:T(8,128)(2,1)}, u32[]{:S(2)}) copy-start(bf16[256,256]{0,1:T(8,128)(2,1)} %copy-done.17) | copy-start | bytes 393220
  129.1 13.3 %collective-permute-start.2 = (bf16[2,256,256]{2,1,0:T(8,128)(2,1)}, bf16[2,256,256]{2,1,0:T(8,128)(2,1)}, u32[]{:S(2)}, u32[]{:S(2)}) collective-permute-start(bf16[2,256,256]{2,1,0:T(8,128)(2,1)} %get-tuple-element.20), channel_id=1, source_target_pairs={{0,1},{1,2},{2,3},{3,48},{48,49},{49,50},{50,51},{51,96},{96,97},{... | collective-permute-start | bytes 786440 | tf_op jit(solution)/shard_map/ppermute | solution.py:18
  131.0 16.3 %collective-permute-start.3 = (bf16[2,256,256]{2,1,0:T(8,128)(2,1)}, bf16[2,256,256]{2,1,0:T(8,128)(2,1)}, u32[]{:S(2)}, u32[]{:S(2)}) collective-permute-start(bf16[2,256,256]{2,1,0:T(8,128)(2,1)} %get-tuple-element.21), channel_id=1, source_target_pairs={{1,0},{2,1},{3,2},{48,3},{49,48},{50,49},{51,50},{96,51},{97,96},{... | collective-permute-start | bytes 786440 | tf_op jit(solution)/shard_map/ppermute | solution.py:20
  (5 other events, 5.3 us)
Sparse Core Ops, SparseCore 0:
  20.5 90.6 all-gather.1
  115.3 272.4 reduce-scatter.4
  391.2 282.0 reduce-scatter.2
where the time goes:
time: 687 us; the launch traced here: 681 us
  waiting for transfers between devices  614 us (89%)
  starting transfers between devices  18.4 us (3%)
  between operations  14.2 us (2%)
  local copies, waits for them, and re-layouts  13.6 us (2%)
  matrix products  13.6 us (2%)
  other arithmetic  7.1 us (1%)
    reduce_scatter x1, waiting for transfers between devices, local(): lax.psum_scatter(key_slots, ('seq', 'rep'), scatter_dimension=0, tiled=True)  284 us
    reduce_scatter x1, waiting for transfers between devices, local(): lax.psum_scatter(value_slots, ('seq', 'rep'), scatter_dimension=0, tiled=...  239 us
    all_gather x1, waiting for transfers between devices, local(): lax.all_gather(grad_output, 'head', axis=1, tiled=True)  77.5 us
    ppermute x2, starting transfers between devices, extended(): lax.ppermute(head, axis, [((i + 1) % count, i) for i in range(ends)])  14.4 us
  transfers between devices with their start and end apart: 7, of which 6 were waited for; matrix products, arithmetic and copies ran while one was open for 4% of the time, Pallas kernels for 0%

commit v1 on v0

v1 whole, which is shorter than its diff:
```python
import functools

import jax
import jax.numpy as jnp
from jax import lax
from jax.experimental import pallas as pl
from jax.experimental.pallas import tpu as pltpu
from jax.sharding import PartitionSpec as P

HD = 128
TILE = 128
CAP = 8
XS = 4
ZS = 3
NEG = -1e30
MESH = pl.DeviceIdType.MESH
F32 = jnp.float32
BF16 = jnp.bfloat16


def dot(a, b, contract):
    return lax.dot_general(a, b, (contract, ((), ())), preferred_element_type=F32)


def kernel(
    seqs,
    reps,
    mask_ref,
    owner_ref,
    q_hbm,
    k_hbm,
    v_hbm,
    g_hbm,
    w_hbm,
    tk_hbm,
    tv_hbm,
    dq_ref,
    dk_ref,
    dv_ref,
    tkg_ref,
    tvg_ref,
    q,
    kall,
    vall,
    gbuf,
    w,
    gacc,
    gh,
    kt,
    st,
    pt,
    dp,
    ds,
    hsend,
    hrecv,
    own,
    place,
    slots,
    trecv1,
    tsum,
    trecv2,
    t3,
    trecv3,
    local_sem,
    zs,
    zr,
    xss,
    xsr,
    xfs,
    xfr,
    hs,
    hr,
    t1s,
    t1r,
    t2s,
    t2r,
    t3s,
    t3r,
):
    seq = lax.axis_index("seq")
    head = lax.axis_index("head")
    rep = lax.axis_index("rep")
    ys = seqs // 2
    y, core = seq // 2, seq % 2
    x, z = head // ZS, head % ZS
    slab = seq * reps + rep
    heads = q.shape[1] // HD
    frame = q.shape[0]
    scale = HD ** (-0.5)

    def head_of(dx, dz):
        return ((x + dx + XS) % XS) * ZS + (z + dz + ZS) % ZS

    z_dev = [{"head": head_of(0, 1)}, {"head": head_of(0, -1)}]
    x_dev = [{"head": head_of(1, 0)}, {"head": head_of(-1, 0)}]
    nxt = (slab + 1) % (seqs * reps)
    prv = (slab + seqs * reps - 1) % (seqs * reps)
    s_dev = [
        {"seq": nxt // reps, "rep": nxt % reps},
        {"seq": prv // reps, "rep": prv % reps},
    ]
    core_dev = {"seq": y * 2 + 1 - core}
    y_dev = [{"seq": ((y + d) % ys) * 2 + core} for d in range(1, ys)]
    r_dev = [{"rep": (rep + d) % reps} for d in range(1, reps)]

    loads = [
        pltpu.make_async_copy(src, dst, local_sem.at[i])
        for i, (src, dst) in enumerate(
            [
                (q_hbm, q),
                (tk_hbm, kall.at[3]),
                (k_hbm, kall.at[1]),
                (g_hbm, gbuf.at[0, 0]),
                (w_hbm, w),
                (tv_hbm, vall.at[3]),
                (v_hbm, vall.at[1]),
            ]
        )
    ]
    for load in loads:
        load.start()

    barrier = pltpu.get_barrier_semaphore()
    partners = z_dev + x_dev + s_dev + [core_dev] + y_dev + r_dev
    for dev in partners:
        pl.semaphore_signal(barrier, inc=1, device_id=dev, device_id_type=MESH)
    pl.semaphore_wait(barrier, len(partners))

    def remote(src, dst, ssem, rsem, dev):
        return pltpu.make_async_remote_copy(
            src_ref=src, dst_ref=dst, send_sem=ssem, recv_sem=rsem, device_id=dev, device_id_type=MESH
        )

    def rows(c):
        return pl.ds(c * TILE, TILE)

    halves = frame // TILE

    zc = [
        [
            remote(g_hbm.at[rows(c)], gbuf.at[0, 1 + d, rows(c)], zs.at[d, c], zr.at[d, c], z_dev[d])
            for c in range(halves)
        ]
        for d in range(2)
    ]
    xc = {}
    xf = {}
    for b in range(3):
        for c in range(halves):
            for d in range(2):
                src = g_hbm.at[rows(c)] if b == 0 else gbuf.at[0, b, rows(c)]
                xc[b, c, d] = remote(
                    src, gbuf.at[1 + d, b, rows(c)], xss.at[d, b, c], xsr.at[d, b, c], x_dev[d]
                )
        for d in range(2):
            xf[b, d] = remote(
                gbuf.at[1 + d, b, rows(d)], gbuf.at[3, b, rows(d)], xfs.at[d, b], xfr.at[d, b], x_dev[d]
            )
    hk = [remote(k_hbm, kall.at[2 * d], hs.at[0, d], hr.at[0, d], s_dev[d]) for d in range(2)]
    hv = [remote(v_hbm, vall.at[2 * d], hs.at[1, d], hr.at[1, d], s_dev[d]) for d in range(2)]
    hg = [
        [
            remote(hsend.at[n, d], hrecv.at[n, d], hs.at[2 + n, d], hr.at[2 + n, d], s_dev[d])
            for d in range(2)
        ]
        for n in range(2)
    ]

    for c in range(halves):
        for d in range(2):
            zc[d][c].start()
    for c in range(halves):
        for d in range(2):
            xc[0, c, d].start()
    for d in range(2):
        hk[d].start()
    for d in range(2):
        hv[d].start()

    def hcols(h):
        return slice(h * HD, (h + 1) * HD)

    lane = lax.broadcasted_iota(jnp.int32, (1, frame), 1)
    tops = [None] * heads

    def scores(j):
        for h in range(heads):
            s = dot(kall[j, :, hcols(h)], q[:, hcols(h)], ((1,), (1,))) * scale
            for t in range(halves):
                part = s[t * TILE : (t + 1) * TILE]
                if j < 3:
                    tile = (slab - 1 + j) * halves + t
                    bias = jnp.zeros((1, frame), F32)
                    for c in range(halves):
                        hit = mask_ref[slab * halves + c, 0] == tile
                        for i in range(1, 3):
                            hit = hit | (mask_ref[slab * halves + c, i] == tile)
                        level = jnp.where(hit, jnp.float32(0.0), jnp.float32(NEG))
                        bias = jnp.where(lane // TILE == c, level, bias)
                    part = part + bias
                st[h, j * frame + t * TILE : j * frame + (t + 1) * TILE, :] = part
                top = jnp.max(part, axis=0, keepdims=True)
                tops[h] = top if tops[h] is None else jnp.maximum(tops[h], top)

    def transposed_keys(j):
        for h in range(heads):
            kt[h, :, j * frame : (j + 1) * frame] = kall[j, :, hcols(h)].T

    loads[0].wait()
    loads[1].wait()
    scores(3)
    loads[2].wait()
    scores(1)

    def forward(b):
        for d in range(2):
            xc[b, d, d].wait_recv()
            xf[b, d].start()

    def add_block(c, xslot, b):
        hd = head_of((0, -1, 1, 2)[xslot], (0, -1, 1)[b])
        cols = pl.ds(pl.multiple_of(hd * frame, frame), frame)
        gacc[rows(c), :] += dot(gbuf[xslot, b, rows(c), :], w[:, cols], ((1,), (1,)))

    forward(0)
    loads[3].wait()
    loads[4].wait()
    gacc[...] = jnp.zeros_like(gacc)
    for c in range(halves):
        add_block(c, 0, 0)

    owner = owner_ref[...]
    texts = owner.shape[1]
    row_i = lax.broadcasted_iota(jnp.int32, (texts, texts), 0)
    col_i = lax.broadcasted_iota(jnp.int32, (texts, texts), 1)
    owner_f = owner.astype(F32)
    owner_col = jnp.sum(jnp.where(row_i == col_i, owner_f, 0.0), axis=1, keepdims=True)
    same = (owner_col == owner_f) & (row_i < col_i)
    rank = jnp.sum(jnp.where(same, 1.0, 0.0), axis=0, keepdims=True).astype(jnp.int32)
    o_rep = owner % reps
    o_seq = owner // reps
    where_to = (((o_seq % 2) * ys + o_seq // 2) * reps + o_rep) * CAP + rank
    slot_i = lax.broadcasted_iota(jnp.int32, place.shape, 0)
    place[...] = jnp.where(slot_i == where_to, 1.0, 0.0).astype(BF16)
    transposed_keys(3)
    transposed_keys(1)

    for c in range(halves):
        for d in range(2):
            zc[d][c].wait_recv()
            for e in range(2):
                xc[1 + d, c, e].start()
        if c == 0:
            for d in range(2):
                xc[0, 1 - d, d].wait_recv()
            for e in range(1, 3):
                for cc in range(halves):
                    add_block(cc, e, 0)
    for b in range(1, 3):
        forward(b)
    for c in range(halves):
        xf[0, c].wait_recv()
        add_block(c, 3, 0)
        for b in range(1, 3):
            add_block(c, 0, b)
    for b in range(1, 3):
        for d in range(2):
            xc[b, 1 - d, d].wait_recv()
            for c in range(halves):
                add_block(c, 1 + d, b)
    for b in range(1, 3):
        for c in range(halves):
            xf[b, c].wait_recv()
            add_block(c, 3, b)
    gh[...] = gacc[...].astype(BF16)

    for d in range(2):
        hk[d].wait_recv()
        scores(2 * d)
    keys_all = st.shape[1]
    for h in range(heads):
        total = jnp.zeros((1, frame), F32)
        for r in range(0, keys_all, TILE):
            e = jnp.exp(st[h, r : r + TILE, :] - tops[h])
            total = total + jnp.sum(e, axis=0, keepdims=True)
            st[h, r : r + TILE, :] = e
        inv = 1.0 / total
        for r in range(0, keys_all, TILE):
            p = st[h, r : r + TILE, :] * inv
            st[h, r : r + TILE, :] = p
            pt[h, r : r + TILE, :] = p.astype(BF16)

    def value_part(j, h):
        return dot(pt[h, j * frame : (j + 1) * frame, :], gh[:, hcols(h)], ((1,), (0,)))

    def key_part(j, h):
        return dot(ds[h, j * frame : (j + 1) * frame, :], q[:, hcols(h)], ((1,), (0,))) * scale

    def text_first(n, part):
        for h in range(heads):
            placed = dot(place[...], part(3, h).astype(BF16), ((1,), (0,)))
            slots[n, :, hcols(h)] = placed.astype(BF16)
        half = slots.shape[1] // 2
        copy = remote(
            slots.at[n, pl.ds((1 - core) * half, half)], trecv1.at[n], t1s.at[n], t1r.at[n], core_dev
        )
        copy.start()
        return copy

    for d in range(2):
        for h in range(heads):
            hsend[0, d, :, hcols(h)] = value_part(2 - 2 * d, h).astype(BF16)
        hg[0][d].start()
    t1 = [None, None]
    t1[0] = text_first(0, value_part)
    for h in range(heads):
        own[0, :, hcols(h)] = value_part(1, h)

    loads[5].wait()
    loads[6].wait()
    delta = [jnp.zeros((1, frame), F32) for _ in range(heads)]

    def dprob(j):
        for h in range(heads):
            for t in range(halves):
                r = j * frame + t * TILE
                part = dot(vall[j, rows(t), hcols(h)], gh[:, hcols(h)], ((1,), (1,)))
                dp[h, r : r + TILE, :] = part
                delta[h] = delta[h] + jnp.sum(
                    pt[h, r : r + TILE, :].astype(F32) * part, axis=0, keepdims=True
                )

    dprob(3)
    dprob(1)

    block = reps * CAP

    def text_second(n):
        t1[n].wait_recv()
        half = trecv1.shape[1]
        mine = slots[n, pl.ds(core * half, half), :].astype(F32)
        tsum[n] = (mine + trecv1[n].astype(F32)).astype(BF16)
        copies = []
        for d in range(1, ys):
            copy = remote(
                tsum.at[n, pl.ds(((y + d) % ys) * block, block)],
                trecv2.at[n, d - 1],
                t2s.at[n, d - 1],
                t2r.at[n, d - 1],
                y_dev[d - 1],
            )
            copy.start()
            copies.append(copy)
        return copies

    def text_third(n, second):
        total = tsum[n, pl.ds(y * block, block), :].astype(F32)
        for d in range(1, ys):
            second[d - 1].wait_recv()
            total = total + trecv2[n, d - 1].astype(F32)
        t3[n] = total
        copies = []
        for d in range(1, reps):
            copy = remote(
                t3.at[n, pl.ds(((rep + d) % reps) * CAP, CAP)],
                trecv3.at[n, d - 1],
                t3s.at[n, d - 1],
                t3r.at[n, d - 1],
                r_dev[d - 1],
            )
            copy.start()
            copies.append(copy)
        return copies

    def text_last(n, third, out):
        total = t3[n, pl.ds(rep * CAP, CAP), :]
        for d in range(1, reps):
            third[d - 1].wait_recv()
            total = total + trecv3[n, d - 1]
        out[...] = total.astype(BF16)

    second = [None, None]
    third = [None, None]
    second[0] = text_second(0)
    for d in range(2):
        transposed_keys(2 * d)
    for d in range(2):
        hv[d].wait_recv()
        dprob(2 * d)

    def dscore(j):
        for h in range(heads):
            for t in range(halves):
                r = j * frame + t * TILE
                ds[h, r : r + TILE, :] = (
                    st[h, r : r + TILE, :] * (dp[h, r : r + TILE, :] - delta[h])
                ).astype(BF16)

    for d in range(2):
        dscore(2 - 2 * d)
        for h in range(heads):
            hsend[1, d, :, hcols(h)] = key_part(2 - 2 * d, h).astype(BF16)
        hg[1][d].start()
    dscore(3)
    t1[1] = text_first(1, key_part)
    dscore(1)
    second[1] = text_second(1)
    for h in range(heads):
        own[1, :, hcols(h)] = key_part(1, h)
    for h in range(heads):
        dqt = dot(kt[h], ds[h], ((1,), (0,))) * scale
        dq_ref[:, hcols(h)] = dqt.T.astype(BF16)
    third[0] = text_third(0, second[0])
    for d in range(2):
        hg[0][d].wait_recv()
    dv_ref[...] = (own[0] + hrecv[0, 0].astype(F32) + hrecv[0, 1].astype(F32)).astype(BF16)
    third[1] = text_third(1, second[1])
    for d in range(2):
        hg[1][d].wait_recv()
    dk_ref[...] = (own[1] + hrecv[1, 0].astype(F32) + hrecv[1, 1].astype(F32)).astype(BF16)
    text_last(0, third[0], tvg_ref)
    text_last(1, third[1], tkg_ref)

    sent = [copy for pair in zc for copy in pair] + list(xc.values()) + list(xf.values())
    sent += hk + hv + hg[0] + hg[1] + t1 + second[0] + second[1] + third[0] + third[1]
    for copy in sent:
        copy.wait_send()


def local(
    seqs,
    reps,
    queries,
    keys,
    values,
    grad_output,
    out_weight,
    text_keys,
    text_values,
    mask_lists,
    text_owner,
):
    frame, width = queries.shape
    texts = text_keys.shape[0]
    heads = width // HD
    ys = seqs // 2
    slots = seqs * reps * CAP
    halves = frame // TILE
    block = reps * CAP
    total = 3 * frame + texts
    grads = jax.ShapeDtypeStruct((frame, width), BF16)
    text_grads = jax.ShapeDtypeStruct((CAP, width), BF16)
    hbm = pl.BlockSpec(memory_space=pl.ANY)
    vmem = pl.BlockSpec(memory_space=pltpu.VMEM)
    dma = pltpu.SemaphoreType.DMA
    return pl.pallas_call(
        functools.partial(kernel, seqs, reps),
        out_shape=(grads, grads, grads, text_grads, text_grads),
        in_specs=[pl.BlockSpec(memory_space=pltpu.SMEM), vmem] + [hbm] * 7,
        out_specs=(vmem,) * 5,
        scratch_shapes=[
            pltpu.VMEM((frame, width), BF16),
            pltpu.VMEM((4, frame, width), BF16),
            pltpu.VMEM((4, frame, width), BF16),
            pltpu.VMEM((XS, ZS, frame, width), BF16),
            pltpu.VMEM(out_weight.shape, BF16),
            pltpu.VMEM((frame, width), F32),
            pltpu.VMEM((frame, width), BF16),
            pltpu.VMEM((heads, HD, total), BF16),
            pltpu.VMEM((heads, total, frame), F32),
            pltpu.VMEM((heads, total, frame), BF16),
            pltpu.VMEM((heads, total, frame), F32),
            pltpu.VMEM((heads, total, frame), BF16),
            pltpu.VMEM((2, 2, frame, width), BF16),
            pltpu.VMEM((2, 2, frame, width), BF16),
            pltpu.VMEM((2, frame, width), F32),
            pltpu.VMEM((slots, texts), BF16),
            pltpu.VMEM((2, slots, width), BF16),
            pltpu.VMEM((2, slots // 2, width), BF16),
            pltpu.VMEM((2, slots // 2, width), BF16),
            pltpu.VMEM((2, ys - 1, block, width), BF16),
            pltpu.VMEM((2, block, width), F32),
            pltpu.VMEM((2, reps - 1, CAP, width), F32),
            dma((7,)),
            dma((2, halves)),
            dma((2, halves)),
            dma((2, 3, halves)),
            dma((2, 3, halves)),
            dma((2, 3)),
            dma((2, 3)),
            dma((4, 2)),
            dma((4, 2)),
            dma((2,)),
            dma((2,)),
            dma((2, ys - 1)),
            dma((2, ys - 1)),
            dma((2, reps - 1)),
            dma((2, reps - 1)),
        ],
        compiler_params=pltpu.CompilerParams(collective_id=0, has_side_effects=True),
    )(
        mask_lists,
        text_owner.reshape(1, texts),
        queries,
        keys,
        values,
        grad_output,
        out_weight,
        text_keys,
        text_values,
    )


def solution(mesh):
    rows = P(("seq", "rep"), "head")
    return jax.shard_map(
        functools.partial(local, mesh.shape["seq"], mesh.shape["rep"]),
        mesh=mesh,
        in_specs=(
            rows,
            rows,
            rows,
            rows,
            P("head", None),
            P(None, "head"),
            P(None, "head"),
            P(),
            P(),
        ),
        out_specs=(rows,) * 5,
        check_vma=False,
    )
```

time: 687 us -> 72.2 us (0.11)
  waiting for transfers between devices: 614 us -> 0 us
  Pallas kernels: 0 us -> 62.5 us
  starting transfers between devices: 18.4 us -> 0 us
  matrix products: 13.6 us -> 0 us
  between operations: 14.2 us -> 0.64 us
  other arithmetic: 7.1 us -> 0 us
    reduce_scatter x2 -> x0, waiting for transfers between devices: 523 us -> none  [the longest x1 284 us: local(): lax.psum_scatter(key_slots, ('seq', 'rep'), scatter_dimension=0, tiled=True)]
    all_gather x1 -> x0, waiting for transfers between devices: 77.5 us -> none  [local(): lax.all_gather(grad_output, 'head', axis=1, tiled=True)]
    pallas_call x0 -> x1, Pallas kernels: none -> 62.5 us  [local(): pl.pallas_call(functools.partial(kernel, seqs, reps), out_shape=(grads, g...]
    ppermute x4 -> x0, starting transfers between devices: 18.3 us -> none  [the longest x2 14.4 us: extended(): lax.ppermute(head, axis, [((i + 1) % count, i) for i in range(ends)])]
    ppermute x4 -> x0, waiting for transfers between devices: 13.8 us -> none  [the longest x2 8.85 us: extended(): lax.ppermute(tail, axis, [(i, (i + 1) % count) for i in range(ends)])]
    dot_general x15 -> x0, matrix products: 13.6 us -> none  [the longest x1 2.07 us: local(): lax.dot_general(lax.all_gather(grad_output, 'head', axis=1, tiled=True),...]
  transfers between devices with their start and end apart: 7 -> 0, of which waited for: 6 -> 0; matrix products, arithmetic and copies ran while one was open for 4% -> 0% of each run, Pallas kernels for 0% -> 0%
where the time goes in v1:
time: 72.2 us; the launch traced here: 71.8 us
  Pallas kernels  62.5 us (87%)
  local copies, waits for them, and re-layouts  8.66 us (12%)
    pallas_call x1, Pallas kernels, local(): pl.pallas_call(functools.partial(kernel, seqs, reps), out_shape=(grads, g...  62.5 us
    unnamed x6, local copies, waits for them, and re-layouts  8.66 us

profile of v1, /device:TPU:1, one launch (start us, length us, event | category | flops | bytes accessed | tf_op | source)
XLA Modules:
  0.0 71.8 jit_solution(10583798614493880950)
XLA Ops:
  0.6 1.4 %copy.14.mask_ref = s32[128,3]{1,0:T(8,128)} copy(s32[128,3]{0,1:T(4,128)} %param.16) | data formatting | bytes 3072 | tf_op args[7]
  2.0 62.5 %shard_map.128 = (bf16[256,256]{1,0:T(8,128)(2,1)}, bf16[256,256]{1,0:T(8,128)(2,1)}, bf16[256,256]{1,0:T(8,128)(2,1)}, bf16[8,256]{1,0:T(8,128)(2,1)}, bf16[8,256]{1,0:T(8,128)(2,1)}) custom-call(s32[128,3]{1,0:T(8,128)} %copy.14.mask_ref, s32[1,256]{1,0:T(1,128)} %bitcast.1, bf16[256,256]{1,0:T(8,128)(2,1)} %q_hbm.1, bf16[256,256]{1,0:T(8,128)(2,1)} %k_hbm.1, ...), custom_call_target="tpu_custom_call" | custom-call | tf_op jit(solution)/shard_map/pallas_call | solution.py:456
  64.5 1.6 %copy.20 = bf16[256,256]{1,0:T(8,128)(2,1)} copy(bf16[256,256]{1,0:T(8,128)(2,1)} %get-tuple-element.10) | data formatting | bytes 262144
  66.1 1.6 %copy.21 = bf16[256,256]{1,0:T(8,128)(2,1)} copy(bf16[256,256]{1,0:T(8,128)(2,1)} %get-tuple-element.11) | data formatting | bytes 262144
  67.7 1.6 %copy.22 = bf16[256,256]{1,0:T(8,128)(2,1)} copy(bf16[256,256]{1,0:T(8,128)(2,1)} %get-tuple-element.12) | data formatting | bytes 262144
  69.3 1.3 %copy.23 = bf16[8,256]{1,0:T(8,128)(2,1)} copy(bf16[8,256]{1,0:T(8,128)(2,1)} %get-tuple-element.13) | data formatting | bytes 8192
  70.5 1.3 %copy.24 = bf16[8,256]{1,0:T(8,128)(2,1)} copy(bf16[8,256]{1,0:T(8,128)(2,1)} %get-tuple-element.14) | data formatting | bytes 8192

commit v2 on v1

v2 whole, which is shorter than its diff:
```python
import functools

import jax
import jax.numpy as jnp
from jax import lax
from jax.experimental import pallas as pl
from jax.experimental.pallas import tpu as pltpu
from jax.sharding import PartitionSpec as P

HD = 128
TILE = 128
CAP = 8
XS = 4
ZS = 3
NEG = -1e30
MESH = pl.DeviceIdType.MESH
F32 = jnp.float32
BF16 = jnp.bfloat16


def dot(a, b, contract):
    return lax.dot_general(a, b, (contract, ((), ())), preferred_element_type=F32)


def kernel(
    seqs,
    reps,
    mask_ref,
    owner_ref,
    q_hbm,
    k_hbm,
    v_hbm,
    g_hbm,
    w_hbm,
    tk_hbm,
    tv_hbm,
    dq_ref,
    dk_ref,
    dv_ref,
    tkg_ref,
    tvg_ref,
    qall,
    kall,
    vall,
    gall,
    gbuf,
    w,
    gacc,
    kt,
    st,
    pt,
    dp,
    ds,
    hp,
    hpt,
    own,
    stat,
    place,
    slots,
    trecv1,
    tsum,
    trecv2,
    t3,
    trecv3,
    ready,
    local_sem,
    zs,
    zr,
    xss,
    xsr,
    xfs,
    xfr,
    hs,
    hr,
    t1s,
    t1r,
    t2s,
    t2r,
    t3s,
    t3r,
):
    seq = lax.axis_index("seq")
    head = lax.axis_index("head")
    rep = lax.axis_index("rep")
    ys = seqs // 2
    y, core = seq // 2, seq % 2
    x, z = head // ZS, head % ZS
    slabs = seqs * reps
    slab = seq * reps + rep
    frame, width = q_hbm.shape
    heads = width // HD
    halves = frame // TILE
    scale = HD ** (-0.5)

    def head_of(dx, dz):
        return ((x + dx + XS) % XS) * ZS + (z + dz + ZS) % ZS

    z_dev = [{"head": head_of(0, 1)}, {"head": head_of(0, -1)}]
    z_of = [(z + 1) % ZS, (z + ZS - 1) % ZS]
    x_dev = [{"head": head_of(1, 0)}, {"head": head_of(-1, 0)}]
    nxt = (slab + 1) % slabs
    prv = (slab + slabs - 1) % slabs
    s_dev = [
        {"seq": nxt // reps, "rep": nxt % reps},
        {"seq": prv // reps, "rep": prv % reps},
    ]
    core_dev = {"seq": y * 2 + 1 - core}
    y_dev = [{"seq": ((y + d) % ys) * 2 + core} for d in range(1, ys)]
    r_dev = [{"rep": (rep + d) % reps} for d in range(1, reps)]

    loads = [
        pltpu.make_async_copy(src, dst, local_sem.at[i])
        for i, (src, dst) in enumerate(
            [
                (q_hbm, qall.at[1]),
                (tk_hbm, kall.at[3]),
                (k_hbm, kall.at[1]),
                (g_hbm, gbuf.at[0, 0]),
                (w_hbm, w),
                (tv_hbm, vall.at[3]),
                (v_hbm, vall.at[1]),
            ]
        )
    ]
    for load in loads:
        load.start()

    for n in range(2):
        stat[n, 1] = jnp.full(stat.shape[2:], NEG, F32)

    barrier = pltpu.get_barrier_semaphore()
    partners = x_dev + s_dev + [core_dev] + y_dev + r_dev
    for dev in partners:
        pl.semaphore_signal(barrier, inc=1, device_id=dev, device_id_type=MESH)
    pl.semaphore_wait(barrier, len(partners) + z)
    for d in range(2):

        @pl.when(z_of[d] > z)
        def _():
            pl.semaphore_signal(barrier, inc=1, device_id=z_dev[d], device_id_type=MESH)

        @pl.when(z_of[d] < z)
        def _():
            pl.semaphore_signal(ready.at[1 - d], inc=1, device_id=z_dev[d], device_id_type=MESH)

    sent = []

    def remote(src, dst, ssem, rsem, dev):
        copy = pltpu.make_async_remote_copy(
            src_ref=src, dst_ref=dst, send_sem=ssem, recv_sem=rsem, device_id=dev, device_id_type=MESH
        )
        sent.append(copy)
        return copy

    def rows(c):
        return pl.ds(c * TILE, TILE)

    def hcols(h):
        return slice(h * HD, (h + 1) * HD)

    zc = [
        [
            remote(g_hbm.at[rows(c)], gbuf.at[0, 1 + d, rows(c)], zs.at[d, c], zr.at[d, c], z_dev[d])
            for c in range(halves)
        ]
        for d in range(2)
    ]
    xc = {}
    xf = {}
    for b in range(3):
        for c in range(halves):
            for d in range(2):
                src = g_hbm.at[rows(c)] if b == 0 else gbuf.at[0, b, rows(c)]
                xc[b, c, d] = remote(
                    src, gbuf.at[1 + d, b, rows(c)], xss.at[d, b, c], xsr.at[d, b, c], x_dev[d]
                )
        for d in range(2):
            xf[b, d] = remote(
                gbuf.at[1 + d, b, rows(d)], gbuf.at[3, b, rows(d)], xfs.at[d, b], xfr.at[d, b], x_dev[d]
            )

    def halo(n, src, dst):
        return [remote(src, dst.at[2 * d], hs.at[n, d], hr.at[n, d], s_dev[d]) for d in range(2)]

    hk = halo(0, k_hbm, kall)
    hv = halo(1, v_hbm, vall)
    hq = halo(2, q_hbm, qall)
    hg = halo(3, gall.at[1], gall)
    ha = halo(4, stat.at[0, 1], stat.at[0])
    hd = halo(5, stat.at[1, 1], stat.at[1])

    def z_send(d):
        for c in range(halves):
            zc[d][c].start()

    def z_send_later(d):
        pl.semaphore_wait(ready.at[d], 1)
        z_send(d)

    for d in range(2):

        @pl.when(z_of[d] < z)
        def _():
            z_send(d)

    for c in range(halves):
        for d in range(2):
            xc[0, c, d].start()
    for copy in hk + hv:
        copy.start()

    lane = lax.broadcasted_iota(jnp.int32, (1, frame), 1)

    def bias_of(tile, of_slab):
        bias = jnp.zeros((1, frame), F32)
        for c in range(halves):
            hit = mask_ref[0, of_slab * halves + c] == tile
            for i in range(1, 3):
                hit = hit | (mask_ref[i, of_slab * halves + c] == tile)
            level = jnp.where(hit, jnp.float32(0.0), jnp.float32(NEG))
            bias = jnp.where(lane // TILE == c, level, bias)
        return bias

    def scores(j):
        for h in range(heads):
            s = dot(kall[j, :, hcols(h)], qall[1, :, hcols(h)], ((1,), (1,))) * scale
            top = stat[0, 1, h : h + 1, :]
            for t in range(halves):
                part = s[t * TILE : (t + 1) * TILE]
                if j < 3:
                    part = part + bias_of((slab - 1 + j) * halves + t, slab)
                st[h, j * frame + t * TILE : j * frame + (t + 1) * TILE, :] = part
                top = jnp.maximum(top, jnp.max(part, axis=0, keepdims=True))
            stat[0, 1, h : h + 1, :] = top

    def transposed_keys(j):
        for h in range(heads):
            kt[h, :, j * frame : (j + 1) * frame] = kall[j, :, hcols(h)].T

    keys_all = st.shape[1]

    def probabilities():
        for d in range(2):
            hk[d].wait_recv()
            scores(2 * d)
        for h in range(heads):
            top = stat[0, 1, h : h + 1, :]
            total = jnp.zeros((1, frame), F32)
            for r in range(0, keys_all, TILE):
                e = jnp.exp(st[h, r : r + TILE, :] - top)
                total = total + jnp.sum(e, axis=0, keepdims=True)
                st[h, r : r + TILE, :] = e
            inv = 1.0 / total
            stat[0, 1, heads + h : heads + h + 1, :] = inv
            for r in range(0, keys_all, TILE):
                p = st[h, r : r + TILE, :] * inv
                st[h, r : r + TILE, :] = p
                pt[h, r : r + TILE, :] = p.astype(BF16)
        for d in range(2):
            ha[d].start()
            transposed_keys(2 * d)

    loads[0].wait()
    loads[1].wait()
    scores(3)
    loads[2].wait()
    scores(1)

    def forward(b):
        for d in range(2):
            xc[b, d, d].wait_recv()
            xf[b, d].start()

    def add_block(c, xslot, b):
        hd_at = head_of((0, -1, 1, 2)[xslot], (0, -1, 1)[b])
        cols = pl.ds(pl.multiple_of(hd_at * frame, frame), frame)
        gacc[rows(c), :] += dot(gbuf[xslot, b, rows(c), :], w[:, cols], ((1,), (1,)))

    forward(0)
    loads[3].wait()
    loads[4].wait()
    gacc[...] = jnp.zeros_like(gacc)
    for c in range(halves):
        add_block(c, 0, 0)

    owner = owner_ref[...]
    texts = owner.shape[1]
    row_i = lax.broadcasted_iota(jnp.int32, (texts, texts), 0)
    col_i = lax.broadcasted_iota(jnp.int32, (texts, texts), 1)
    owner_f = owner.astype(F32)
    owner_col = jnp.sum(jnp.where(row_i == col_i, owner_f, 0.0), axis=1, keepdims=True)
    same = (owner_col == owner_f) & (row_i < col_i)
    rank = jnp.sum(jnp.where(same, 1.0, 0.0), axis=0, keepdims=True).astype(jnp.int32)
    o_rep = owner % reps
    o_seq = owner // reps
    where_to = (((o_seq % 2) * ys + o_seq // 2) * reps + o_rep) * CAP + rank
    slot_i = lax.broadcasted_iota(jnp.int32, place.shape, 0)
    place[...] = jnp.where(slot_i == where_to, 1.0, 0.0).astype(BF16)
    transposed_keys(3)
    transposed_keys(1)

    @pl.when(z == 0)
    def _():
        z_send_later(0)
        probabilities()
        z_send_later(1)

    @pl.when(z == 1)
    def _():
        z_send_later(0)

    for copy in hq:
        copy.start()

    @pl.when(z == 1)
    def _():
        probabilities()

    for d in range(2):
        xc[0, 1 - d, d].wait_recv()
    for e in range(1, 3):
        for c in range(halves):
            add_block(c, e, 0)
    for c in range(halves):
        xf[0, c].wait_recv()
        add_block(c, 3, 0)
    for c in range(halves):
        for d in range(2):
            zc[d][c].wait_recv()
            for e in range(2):
                xc[1 + d, c, e].start()
    for b in range(1, 3):
        forward(b)
    for c in range(halves):
        for b in range(1, 3):
            add_block(c, 0, b)
    for b in range(1, 3):
        for d in range(2):
            xc[b, 1 - d, d].wait_recv()
            for c in range(halves):
                add_block(c, 1 + d, b)
    for b in range(1, 3):
        for c in range(halves):
            xf[b, c].wait_recv()
            add_block(c, 3, b)
    gall[1] = gacc[...].astype(BF16)
    for copy in hg:
        copy.start()

    @pl.when(z == 2)
    def _():
        probabilities()

    def value_part(j, h):
        return dot(pt[h, j * frame : (j + 1) * frame, :], gall[1, :, hcols(h)], ((1,), (0,)))

    def key_part(j, h):
        return dot(ds[h, j * frame : (j + 1) * frame, :], qall[1, :, hcols(h)], ((1,), (0,)))

    half = slots.shape[1] // 2
    block = reps * CAP
    first = [
        remote(slots.at[n, pl.ds((1 - core) * half, half)], trecv1.at[n], t1s.at[n], t1r.at[n], core_dev)
        for n in range(2)
    ]
    second = [
        [
            remote(
                tsum.at[n, pl.ds(((y + d) % ys) * block, block)],
                trecv2.at[n, d - 1],
                t2s.at[n, d - 1],
                t2r.at[n, d - 1],
                y_dev[d - 1],
            )
            for d in range(1, ys)
        ]
        for n in range(2)
    ]
    third = [
        [
            remote(
                t3.at[n, pl.ds(((rep + d) % reps) * CAP, CAP)],
                trecv3.at[n, d - 1],
                t3s.at[n, d - 1],
                t3r.at[n, d - 1],
                r_dev[d - 1],
            )
            for d in range(1, reps)
        ]
        for n in range(2)
    ]

    def text_first(n, part):
        for h in range(heads):
            placed = dot(place[...], part(3, h).astype(BF16), ((1,), (0,)))
            slots[n, :, hcols(h)] = placed.astype(BF16)
        first[n].start()

    def text_second(n):
        first[n].wait_recv()
        mine = slots[n, pl.ds(core * half, half), :].astype(F32)
        tsum[n] = (mine + trecv1[n].astype(F32)).astype(BF16)
        for copy in second[n]:
            copy.start()

    def text_third(n):
        total = tsum[n, pl.ds(y * block, block), :].astype(F32)
        for d in range(1, ys):
            second[n][d - 1].wait_recv()
            total = total + trecv2[n, d - 1].astype(F32)
        t3[n] = total
        for copy in third[n]:
            copy.start()

    def text_last(n, out):
        total = t3[n, pl.ds(rep * CAP, CAP), :]
        for d in range(1, reps):
            third[n][d - 1].wait_recv()
            total = total + trecv3[n, d - 1]
        out[...] = total.astype(BF16)

    delta = [jnp.zeros((1, frame), F32) for _ in range(heads)]

    def dprob(j):
        for h in range(heads):
            for t in range(halves):
                r = j * frame + t * TILE
                part = dot(vall[j, rows(t), hcols(h)], gall[1, :, hcols(h)], ((1,), (1,)))
                dp[h, r : r + TILE, :] = part
                delta[h] = delta[h] + jnp.sum(
                    pt[h, r : r + TILE, :].astype(F32) * part, axis=0, keepdims=True
                )

    def dscore(j):
        for h in range(heads):
            for t in range(halves):
                r = j * frame + t * TILE
                ds[h, r : r + TILE, :] = (
                    st[h, r : r + TILE, :] * (dp[h, r : r + TILE, :] - delta[h])
                ).astype(BF16)

    text_first(0, value_part)
    loads[5].wait()
    loads[6].wait()
    dprob(3)
    dprob(1)
    for d in range(2):
        hv[d].wait_recv()
        dprob(2 * d)
    for h in range(heads):
        stat[1, 1, h : h + 1, :] = delta[h]
    for copy in hd:
        copy.start()
    dscore(3)
    text_first(1, lambda j, h: key_part(j, h) * scale)
    text_second(0)
    for h in range(heads):
        own[0, :, hcols(h)] = value_part(1, h)
    dscore(1)
    text_second(1)
    dscore(0)
    dscore(2)
    for h in range(heads):
        own[1, :, hcols(h)] = key_part(1, h)
    for h in range(heads):
        dqt = dot(kt[h], ds[h], ((1,), (0,))) * scale
        dq_ref[:, hcols(h)] = dqt.T.astype(BF16)

    for d in range(2):
        hq[d].wait_recv()
        ha[d].wait_recv()
        for h in range(heads):
            s = dot(kall[1, :, hcols(h)], qall[2 * d, :, hcols(h)], ((1,), (1,))) * scale
            top = stat[0, 2 * d, h : h + 1, :]
            inv = stat[0, 2 * d, heads + h : heads + h + 1, :]
            for t in range(halves):
                part = s[t * TILE : (t + 1) * TILE] + bias_of(slab * halves + t, (prv, nxt)[d])
                p = jnp.exp(part - top) * inv
                hp[d, h, rows(t), :] = p
                hpt[d, h, rows(t), :] = p.astype(BF16)
    text_third(0)
    for d in range(2):
        hd[d].wait_recv()
        hg[d].wait_recv()
        for h in range(heads):
            g = gall[2 * d, :, hcols(h)]
            own[0, :, hcols(h)] += dot(hpt[d, h], g, ((1,), (0,)))
            dph = dot(vall[1, :, hcols(h)], g, ((1,), (1,)))
            dsh = (hp[d, h] * (dph - stat[1, 2 * d, h : h + 1, :])).astype(BF16)
            own[1, :, hcols(h)] += dot(dsh, qall[2 * d, :, hcols(h)], ((1,), (0,)))
    dv_ref[...] = own[0].astype(BF16)
    dk_ref[...] = (own[1] * scale).astype(BF16)
    text_third(1)
    text_last(0, tvg_ref)
    text_last(1, tkg_ref)

    for copy in sent:
        copy.wait_send()


def hand_over(*refs):
    count = (len(refs) - 2) // 3
    given, taken, held = refs[:count], refs[count : 2 * count], refs[2 * count : 3 * count]
    in_sem, out_sem = refs[3 * count :]
    ins = [pltpu.make_async_copy(given[i], held[i], in_sem.at[i]) for i in range(count)]
    outs = [pltpu.make_async_copy(held[i], taken[i], out_sem.at[i]) for i in range(count)]
    for copy in ins:
        copy.start()
    for i in range(count):
        ins[i].wait()
        outs[i].start()
    for copy in outs:
        copy.wait()


def local(
    seqs,
    reps,
    queries,
    keys,
    values,
    grad_output,
    out_weight,
    text_keys,
    text_values,
    mask_lists,
    text_owner,
):
    frame, width = queries.shape
    texts = text_keys.shape[0]
    heads = width // HD
    ys = seqs // 2
    slots = seqs * reps * CAP
    halves = frame // TILE
    block = reps * CAP
    total = 3 * frame + texts
    grads = jax.ShapeDtypeStruct((frame, width), BF16)
    text_grads = jax.ShapeDtypeStruct((CAP, width), BF16)
    hbm = pl.BlockSpec(memory_space=pltpu.HBM)
    vmem = pl.BlockSpec(memory_space=pltpu.VMEM)
    dma = pltpu.SemaphoreType.DMA
    shapes = (grads, grads, grads, text_grads, text_grads)
    made = pl.pallas_call(
        functools.partial(kernel, seqs, reps),
        out_shape=shapes,
        in_specs=[pl.BlockSpec(memory_space=pltpu.SMEM), vmem] + [hbm] * 7,
        out_specs=(vmem,) * 5,
        scratch_shapes=[
            pltpu.VMEM((3, frame, width), BF16),
            pltpu.VMEM((4, frame, width), BF16),
            pltpu.VMEM((4, frame, width), BF16),
            pltpu.VMEM((3, frame, width), BF16),
            pltpu.VMEM((XS, ZS, frame, width), BF16),
            pltpu.VMEM(out_weight.shape, BF16),
            pltpu.VMEM((frame, width), F32),
            pltpu.VMEM((heads, HD, total), BF16),
            pltpu.VMEM((heads, total, frame), F32),
            pltpu.VMEM((heads, total, frame), BF16),
            pltpu.VMEM((heads, total, frame), F32),
            pltpu.VMEM((heads, total, frame), BF16),
            pltpu.VMEM((2, heads, frame, frame), F32),
            pltpu.VMEM((2, heads, frame, frame), BF16),
            pltpu.VMEM((2, frame, width), F32),
            pltpu.VMEM((2, 3, 8, frame), F32),
            pltpu.VMEM((slots, texts), BF16),
            pltpu.VMEM((2, slots, width), BF16),
            pltpu.VMEM((2, slots // 2, width), BF16),
            pltpu.VMEM((2, slots // 2, width), BF16),
            pltpu.VMEM((2, ys - 1, block, width), BF16),
            pltpu.VMEM((2, block, width), F32),
            pltpu.VMEM((2, reps - 1, CAP, width), F32),
            pltpu.SemaphoreType.REGULAR((2,)),
            dma((7,)),
            dma((2, halves)),
            dma((2, halves)),
            dma((2, 3, halves)),
            dma((2, 3, halves)),
            dma((2, 3)),
            dma((2, 3)),
            dma((6, 2)),
            dma((6, 2)),
            dma((2,)),
            dma((2,)),
            dma((2, ys - 1)),
            dma((2, ys - 1)),
            dma((2, reps - 1)),
            dma((2, reps - 1)),
        ],
        compiler_params=pltpu.CompilerParams(collective_id=0, has_side_effects=True),
    )(
        mask_lists.T,
        text_owner.reshape(1, texts),
        queries,
        keys,
        values,
        grad_output,
        out_weight,
        text_keys,
        text_values,
    )
    return pl.pallas_call(
        hand_over,
        out_shape=shapes,
        in_specs=[pl.BlockSpec(memory_space=pl.ANY)] * 5,
        out_specs=(pl.BlockSpec(memory_space=pl.ANY),) * 5,
        scratch_shapes=[pltpu.VMEM(s.shape, s.dtype) for s in shapes] + [dma((5,)), dma((5,))],
    )(*made)


def solution(mesh):
    rows = P(("seq", "rep"), "head")
    return jax.shard_map(
        functools.partial(local, mesh.shape["seq"], mesh.shape["rep"]),
        mesh=mesh,
        in_specs=(
            rows,
            rows,
            rows,
            rows,
            P("head", None),
            P(None, "head"),
            P(None, "head"),
            P(),
            P(),
        ),
        out_specs=(rows,) * 5,
        check_vma=False,
    )
```

time: 72.2 us -> 63.6 us (0.88)
  the two profiles are of different devices: /device:TPU:1 before, /device:TPU:706 now
where the time goes in v2:
time: 63.6 us; the launch traced here: 63.4 us
  Pallas kernels  62.8 us (99%)
  between operations  0.64 us (1%)
    pallas_call x1, Pallas kernels, local(): pl.pallas_call(functools.partial(kernel, seqs, reps), out_shape=shapes, i...  61 us
    pallas_call x1, Pallas kernels, local(): pl.pallas_call(hand_over, out_shape=shapes, in_specs=[pl.BlockSpec(memory...  1.78 us

profile of v2, /device:TPU:706, one launch (start us, length us, event | category | flops | bytes accessed | tf_op | source)
XLA Modules:
  0.0 63.4 jit_solution(11833638421500290338)
XLA Ops:
  0.6 61.0 %shard_map.128 = (bf16[256,256]{1,0:T(8,128)(2,1)}, bf16[256,256]{1,0:T(8,128)(2,1)}, bf16[256,256]{1,0:T(8,128)(2,1)}, bf16[8,256]{1,0:T(8,128)(2,1)}, bf16[8,256]{1,0:T(8,128)(2,1)}) custom-call(s32[3,128]{1,0:T(4,128)} %bitcast.2, s32[1,256]{1,0:T(1,128)} %bitcast.3, bf16[256,256]{1,0:T(8,128)(2,1)} %q_hbm.1, bf16[256,256]{1,0:T(8,128)(2,1)} %k_hbm.1, ...), custom_call_target="tpu_custom_call" | custom-call | tf_op jit(solution)/shard_map/pallas_call | solution.py:543
  61.7 1.8 %shard_map.129 = (bf16[256,256]{1,0:T(8,128)(2,1)}, bf16[256,256]{1,0:T(8,128)(2,1)}, bf16[256,256]{1,0:T(8,128)(2,1)}, bf16[8,256]{1,0:T(8,128)(2,1)}, bf16[8,256]{1,0:T(8,128)(2,1)}) custom-call(bf16[256,256]{1,0:T(8,128)(2,1)} %get-tuple-element.10.refs_0_, bf16[256,256]{1,0:T(8,128)(2,1)} %get-tuple-element.11.refs_1_, ...), custom_call_target="tpu_custom_call" | custom-call | tf_op jit(solution)/shard_map/pallas_call | solution.py:601

commit v3 on v2

--- a/solution.py
+++ b/solution.py
@@ -10,6 +10,7 @@
 HD = 128
 TILE = 128
 CAP = 8
+CHUNKS = 4
 XS = 4
 ZS = 3
 NEG = -1e30
@@ -62,7 +63,9 @@
     trecv2,
     t3,
     trecv3,
-    ready,
+    ready_z,
+    ready_s,
+    ready_r,
     local_sem,
     zs,
     zr,
@@ -128,20 +131,29 @@
     for n in range(2):
         stat[n, 1] = jnp.full(stat.shape[2:], NEG, F32)
 
+    s_rep = [nxt % reps, prv % reps]
+    r_rep = [(rep + d) % reps for d in range(1, reps)]
+    across = [(z_dev[d], z_of[d] - z, ready_z.at[1 - d]) for d in range(2)]
+    across += [(s_dev[d], s_rep[d] - rep, ready_s.at[1 - d]) for d in range(2)]
+    across += [(r_dev[d - 1], r_rep[d - 1] - rep, ready_r.at[reps - d - 1]) for d in range(1, reps)]
     barrier = pltpu.get_barrier_semaphore()
-    partners = x_dev + s_dev + [core_dev] + y_dev + r_dev
+    partners = x_dev + [core_dev] + y_dev
     for dev in partners:
         pl.semaphore_signal(barrier, inc=1, device_id=dev, device_id_type=MESH)
-    pl.semaphore_wait(barrier, len(partners) + z)
-    for d in range(2):
-
-        @pl.when(z_of[d] > z)
+    expected = len(partners)
+    for dev, above, _ in across:
+        expected = expected + jnp.where(above < 0, 1, 0)
+
+        @pl.when(above > 0)
         def _():
-            pl.semaphore_signal(barrier, inc=1, device_id=z_dev[d], device_id_type=MESH)
-
-        @pl.when(z_of[d] < z)
+            pl.semaphore_signal(barrier, inc=1, device_id=dev, device_id_type=MESH)
+
+    pl.semaphore_wait(barrier, expected)
+    for dev, above, sem in across:
+
+        @pl.when(above < 0)
         def _():
-            pl.semaphore_signal(ready.at[1 - d], inc=1, device_id=z_dev[d], device_id_type=MESH)
+            pl.semaphore_signal(sem, inc=1, device_id=dev, device_id_type=MESH)
 
     sent = []
 
@@ -158,25 +170,30 @@
     def hcols(h):
         return slice(h * HD, (h + 1) * HD)
 
+    step = frame // CHUNKS
+
+    def part(c):
+        return pl.ds(c * step, step)
+
     zc = [
         [
-            remote(g_hbm.at[rows(c)], gbuf.at[0, 1 + d, rows(c)], zs.at[d, c], zr.at[d, c], z_dev[d])
-            for c in range(halves)
+            remote(g_hbm.at[part(c)], gbuf.at[0, 1 + d, part(c)], zs.at[d, c], zr.at[d, c], z_dev[d])
+            for c in range(CHUNKS)
         ]
         for d in range(2)
     ]
     xc = {}
     xf = {}
     for b in range(3):
-        for c in range(halves):
+        for c in range(CHUNKS):
             for d in range(2):
-                src = g_hbm.at[rows(c)] if b == 0 else gbuf.at[0, b, rows(c)]
+                src = g_hbm.at[part(c)] if b == 0 else gbuf.at[0, b, part(c)]
                 xc[b, c, d] = remote(
-                    src, gbuf.at[1 + d, b, rows(c)], xss.at[d, b, c], xsr.at[d, b, c], x_dev[d]
+                    src, gbuf.at[1 + d, b, part(c)], xss.at[d, b, c], xsr.at[d, b, c], x_dev[d]
                 )
-        for d in range(2):
-            xf[b, d] = remote(
-                gbuf.at[1 + d, b, rows(d)], gbuf.at[3, b, rows(d)], xfs.at[d, b], xfr.at[d, b], x_dev[d]
+            d = c % 2
+            xf[b, c] = remote(
+                gbuf.at[1 + d, b, part(c)], gbuf.at[3, b, part(c)], xfs.at[b, c], xfr.at[b, c], x_dev[d]
             )
 
     def halo(n, src, dst):
@@ -190,11 +207,11 @@
     hd = halo(5, stat.at[1, 1], stat.at[1])
 
     def z_send(d):
-        for c in range(halves):
+        for c in range(CHUNKS):
             zc[d][c].start()
 
     def z_send_later(d):
-        pl.semaphore_wait(ready.at[d], 1)
+        pl.semaphore_wait(ready_z.at[d], 1)
         z_send(d)
 
     for d in range(2):
@@ -203,11 +220,9 @@
         def _():
             z_send(d)
 
-    for c in range(halves):
+    for c in range(CHUNKS):
         for d in range(2):
             xc[0, c, d].start()
-    for copy in hk + hv:
-        copy.start()
 
     lane = lax.broadcasted_iota(jnp.int32, (1, frame), 1)
 
@@ -266,22 +281,58 @@
     loads[2].wait()
     scores(1)
 
-    def forward(b):
-        for d in range(2):
-            xc[b, d, d].wait_recv()
-            xf[b, d].start()
-
-    def add_block(c, xslot, b):
+    for d in range(2):
+
+        @pl.when(s_rep[d] > rep)
+        def _():
+            pl.semaphore_wait(ready_s.at[d], 1)
+
+    @pl.when(z < ZS - 1)
+    def _():
+        for copy in hk + hv:
+            copy.start()
+
+    def forward(b, c):
+        xc[b, c, c % 2].wait_recv()
+        xf[b, c].start()
+
+    def add_block(xslot, b):
         hd_at = head_of((0, -1, 1, 2)[xslot], (0, -1, 1)[b])
         cols = pl.ds(pl.multiple_of(hd_at * frame, frame), frame)
-        gacc[rows(c), :] += dot(gbuf[xslot, b, rows(c), :], w[:, cols], ((1,), (1,)))
-
-    forward(0)
+        gacc[...] += dot(gbuf[xslot, b], w[:, cols], ((1,), (1,)))
+
+    def pump(blocks, after):
+        for c in range(CHUNKS):
+            for b in blocks:
+                zc[b - 1][c].wait_recv()
+                for d in range(2):
+                    xc[b, c, d].start()
+            if c > 0:
+                for b in blocks:
+                    forward(b, c - 1)
+            for copy in after.get(c, ()):
+                copy.start()
+        for b in blocks:
+            forward(b, CHUNKS - 1)
+
+    def drain(b):
+        if b > 0:
+            add_block(0, b)
+        for d in range(2):
+            for c in range(CHUNKS):
+                if c % 2 != d:
+                    xc[b, c, d].wait_recv()
+            add_block(1 + d, b)
+        for c in range(CHUNKS):
+            xf[b, c].wait_recv()
+        add_block(3, b)
+
+    for c in range(CHUNKS):
+        forward(0, c)
     loads[3].wait()
     loads[4].wait()
     gacc[...] = jnp.zeros_like(gacc)
-    for c in range(halves):
-        add_block(c, 0, 0)
+    add_block(0, 0)
 
     owner = owner_ref[...]
     texts = owner.shape[1]
@@ -304,45 +355,35 @@
         z_send_later(0)
         probabilities()
         z_send_later(1)
+        for copy in hq:
+            copy.start()
+        drain(0)
+        pump([2], {})
+        drain(2)
+        pump([1], {})
+        drain(1)
 
     @pl.when(z == 1)
     def _():
         z_send_later(0)
-
-    for copy in hq:
-        copy.start()
-
-    @pl.when(z == 1)
+        for copy in hq:
+            copy.start()
+        probabilities()
+        drain(0)
+        pump([1], {})
+        drain(1)
+        pump([2], {})
+        drain(2)
+
+    @pl.when(z == 2)
     def _():
-        probabilities()
-
-    for d in range(2):
-        xc[0, 1 - d, d].wait_recv()
-    for e in range(1, 3):
-        for c in range(halves):
-            add_block(c, e, 0)
-    for c in range(halves):
-        xf[0, c].wait_recv()
-        add_block(c, 3, 0)
-    for c in range(halves):
-        for d in range(2):
-            zc[d][c].wait_recv()
-            for e in range(2):
-                xc[1 + d, c, e].start()
-    for b in range(1, 3):
-        forward(b)
-    for c in range(halves):
-        for b in range(1, 3):
-            add_block(c, 0, b)
-    for b in range(1, 3):
-        for d in range(2):
-            xc[b, 1 - d, d].wait_recv()
-            for c in range(halves):
-                add_block(c, 1 + d, b)
-    for b in range(1, 3):
-        for c in range(halves):
-            xf[b, c].wait_recv()
-            add_block(c, 3, b)
+        drain(0)
+        pump([1, 2], {1: hk, 3: hv})
+        drain(1)
+        drain(2)
+        for copy in hq:
+            copy.start()
+
     gall[1] = gacc[...].astype(BF16)
     for copy in hg:
         copy.start()
@@ -390,11 +431,14 @@
         for n in range(2)
     ]
 
-    def text_first(n, part):
-        for h in range(heads):
-            placed = dot(place[...], part(3, h).astype(BF16), ((1,), (0,)))
-            slots[n, :, hcols(h)] = placed.astype(BF16)
-        first[n].start()
+    def text_first(n, made):
+        halved = [made(3, h).astype(BF16) for h in range(heads)]
+        for k in (1 - core, core):
+            to = pl.ds(pl.multiple_of(k * half, half), half)
+            for h in range(heads):
+                slots[n, to, hcols(h)] = dot(place[to, :], halved[h], ((1,), (0,))).astype(BF16)
+            if k is not core:
+                first[n].start()
 
     def text_second(n):
         first[n].wait_recv()
@@ -409,6 +453,13 @@
             second[n][d - 1].wait_recv()
             total = total + trecv2[n, d - 1].astype(F32)
         t3[n] = total
+        if n == 0:
+            for d in range(1, reps):
+
+                @pl.when(r_rep[d - 1] > rep)
+                def _():
+                    pl.semaphore_wait(ready_r.at[d - 1], 1)
+
         for copy in third[n]:
             copy.start()
 
@@ -531,7 +582,6 @@
     heads = width // HD
     ys = seqs // 2
     slots = seqs * reps * CAP
-    halves = frame // TILE
     block = reps * CAP
     total = 3 * frame + texts
     grads = jax.ShapeDtypeStruct((frame, width), BF16)
@@ -570,13 +620,15 @@
             pltpu.VMEM((2, block, width), F32),
             pltpu.VMEM((2, reps - 1, CAP, width), F32),
             pltpu.SemaphoreType.REGULAR((2,)),
+            pltpu.SemaphoreType.REGULAR((2,)),
+            pltpu.SemaphoreType.REGULAR((reps - 1,)),
             dma((7,)),
-            dma((2, halves)),
-            dma((2, halves)),
-            dma((2, 3, halves)),
-            dma((2, 3, halves)),
-            dma((2, 3)),
-            dma((2, 3)),
+            dma((2, CHUNKS)),
+            dma((2, CHUNKS)),
+            dma((2, 3, CHUNKS)),
+            dma((2, 3, CHUNKS)),
+            dma((3, CHUNKS)),
+            dma((3, CHUNKS)),
             dma((6, 2)),
             dma((6, 2)),
             dma((2,)),

time: 63.6 us -> 74.2 us (1.17)
  the two profiles are of different devices: /device:TPU:706 before, /device:TPU:512 now
where the time goes in v3:
time: 74.2 us; the launch traced here: 74 us
  Pallas kernels  73.3 us (99%)
    pallas_call x1, Pallas kernels, local(): pl.pallas_call(functools.partial(kernel, seqs, reps), out_shape=shapes, i...  71.6 us
    pallas_call x1, Pallas kernels, local(): pl.pallas_call(hand_over, out_shape=shapes, in_specs=[pl.BlockSpec(memory...  1.78 us

profile of v3, /device:TPU:512, one launch (start us, length us, event | category | flops | bytes accessed | tf_op | source)
XLA Modules:
  0.0 74.0 jit_solution(6783673327259226102)
XLA Ops:
  0.6 71.6 %shard_map.128 = (bf16[256,256]{1,0:T(8,128)(2,1)}, bf16[256,256]{1,0:T(8,128)(2,1)}, bf16[256,256]{1,0:T(8,128)(2,1)}, bf16[8,256]{1,0:T(8,128)(2,1)}, bf16[8,256]{1,0:T(8,128)(2,1)}) custom-call(s32[3,128]{1,0:T(4,128)} %bitcast.2, s32[1,256]{1,0:T(1,128)} %bitcast.3, bf16[256,256]{1,0:T(8,128)(2,1)} %q_hbm.1, bf16[256,256]{1,0:T(8,128)(2,1)} %k_hbm.1, ...), custom_call_target="tpu_custom_call" | custom-call | tf_op jit(solution)/shard_map/pallas_call | solution.py:593
  72.2 1.8 %shard_map.129 = (bf16[256,256]{1,0:T(8,128)(2,1)}, bf16[256,256]{1,0:T(8,128)(2,1)}, bf16[256,256]{1,0:T(8,128)(2,1)}, bf16[8,256]{1,0:T(8,128)(2,1)}, bf16[8,256]{1,0:T(8,128)(2,1)}) custom-call(bf16[256,256]{1,0:T(8,128)(2,1)} %get-tuple-element.10.refs_0_, bf16[256,256]{1,0:T(8,128)(2,1)} %get-tuple-element.11.refs_1_, ...), custom_call_target="tpu_custom_call" | custom-call | tf_op jit(solution)/shard_map/pallas_call | solution.py:653

commit v4 on v2

--- a/solution.py
+++ b/solution.py
@@ -49,7 +49,8 @@
     kt,
     st,
     pt,
-    dp,
+    vt,
+    att,
     ds,
     hp,
     hpt,
@@ -158,6 +159,8 @@
     def hcols(h):
         return slice(h * HD, (h + 1) * HD)
 
+    hrows = hcols
+
     zc = [
         [
             remote(g_hbm.at[rows(c)], gbuf.at[0, 1 + d, rows(c)], zs.at[d, c], zr.at[d, c], z_dev[d])
@@ -274,7 +277,7 @@
     def add_block(c, xslot, b):
         hd_at = head_of((0, -1, 1, 2)[xslot], (0, -1, 1)[b])
         cols = pl.ds(pl.multiple_of(hd_at * frame, frame), frame)
-        gacc[rows(c), :] += dot(gbuf[xslot, b, rows(c), :], w[:, cols], ((1,), (1,)))
+        gacc[:, c * TILE : (c + 1) * TILE] += dot(w[:, cols], gbuf[xslot, b, rows(c), :], ((1,), (1,)))
 
     forward(0)
     loads[3].wait()
@@ -329,11 +332,23 @@
             zc[d][c].wait_recv()
             for e in range(2):
                 xc[1 + d, c, e].start()
+    @pl.when(z == 2)
+    def _():
+        probabilities()
+
     for b in range(1, 3):
         forward(b)
     for c in range(halves):
         for b in range(1, 3):
             add_block(c, 0, b)
+    loads[5].wait()
+    loads[6].wait()
+    for d in range(2):
+        hv[d].wait_recv()
+    for h in range(heads):
+        for j in range(4):
+            vt[h, :, j * frame : (j + 1) * frame] = vall[j, :, hcols(h)].T
+        att[h] = dot(vt[h], pt[h], ((1,), (0,)))
     for b in range(1, 3):
         for d in range(2):
             xc[b, 1 - d, d].wait_recv()
@@ -347,12 +362,8 @@
     for copy in hg:
         copy.start()
 
-    @pl.when(z == 2)
-    def _():
-        probabilities()
-
     def value_part(j, h):
-        return dot(pt[h, j * frame : (j + 1) * frame, :], gall[1, :, hcols(h)], ((1,), (0,)))
+        return dot(pt[h, j * frame : (j + 1) * frame, :], gall[1, hrows(h), :], ((1,), (1,)))
 
     def key_part(j, h):
         return dot(ds[h, j * frame : (j + 1) * frame, :], qall[1, :, hcols(h)], ((1,), (0,)))
@@ -400,8 +411,8 @@
         first[n].wait_recv()
         mine = slots[n, pl.ds(core * half, half), :].astype(F32)
         tsum[n] = (mine + trecv1[n].astype(F32)).astype(BF16)
-        for copy in second[n]:
-            copy.start()
+        for d in sorted(range(1, ys), key=lambda d: -min(d, ys - d)):
+            second[n][d - 1].start()
 
     def text_third(n):
         total = tsum[n, pl.ds(y * block, block), :].astype(F32)
@@ -419,45 +430,28 @@
             total = total + trecv3[n, d - 1]
         out[...] = total.astype(BF16)
 
-    delta = [jnp.zeros((1, frame), F32) for _ in range(heads)]
-
-    def dprob(j):
-        for h in range(heads):
-            for t in range(halves):
-                r = j * frame + t * TILE
-                part = dot(vall[j, rows(t), hcols(h)], gall[1, :, hcols(h)], ((1,), (1,)))
-                dp[h, r : r + TILE, :] = part
-                delta[h] = delta[h] + jnp.sum(
-                    pt[h, r : r + TILE, :].astype(F32) * part, axis=0, keepdims=True
-                )
+    delta = []
+    for h in range(heads):
+        delta.append(jnp.sum(gall[1, hrows(h), :].astype(F32) * att[h], axis=0, keepdims=True))
+        stat[1, 1, h : h + 1, :] = delta[h]
+    for copy in hd:
+        copy.start()
 
     def dscore(j):
         for h in range(heads):
             for t in range(halves):
                 r = j * frame + t * TILE
-                ds[h, r : r + TILE, :] = (
-                    st[h, r : r + TILE, :] * (dp[h, r : r + TILE, :] - delta[h])
-                ).astype(BF16)
+                part = dot(vall[j, rows(t), hcols(h)], gall[1, hrows(h), :], ((1,), (0,)))
+                ds[h, r : r + TILE, :] = (st[h, r : r + TILE, :] * (part - delta[h])).astype(BF16)
 
     text_first(0, value_part)
-    loads[5].wait()
-    loads[6].wait()
-    dprob(3)
-    dprob(1)
-    for d in range(2):
-        hv[d].wait_recv()
-        dprob(2 * d)
-    for h in range(heads):
-        stat[1, 1, h : h + 1, :] = delta[h]
-    for copy in hd:
-        copy.start()
     dscore(3)
     text_first(1, lambda j, h: key_part(j, h) * scale)
     text_second(0)
+    dscore(1)
+    text_second(1)
     for h in range(heads):
         own[0, :, hcols(h)] = value_part(1, h)
-    dscore(1)
-    text_second(1)
     dscore(0)
     dscore(2)
     for h in range(heads):
@@ -465,6 +459,7 @@
     for h in range(heads):
         dqt = dot(kt[h], ds[h], ((1,), (0,))) * scale
         dq_ref[:, hcols(h)] = dqt.T.astype(BF16)
+    text_third(0)
 
     for d in range(2):
         hq[d].wait_recv()
@@ -478,19 +473,18 @@
                 p = jnp.exp(part - top) * inv
                 hp[d, h, rows(t), :] = p
                 hpt[d, h, rows(t), :] = p.astype(BF16)
-    text_third(0)
+    text_third(1)
     for d in range(2):
         hd[d].wait_recv()
         hg[d].wait_recv()
         for h in range(heads):
-            g = gall[2 * d, :, hcols(h)]
-            own[0, :, hcols(h)] += dot(hpt[d, h], g, ((1,), (0,)))
-            dph = dot(vall[1, :, hcols(h)], g, ((1,), (1,)))
+            g = gall[2 * d, hrows(h), :]
+            own[0, :, hcols(h)] += dot(hpt[d, h], g, ((1,), (1,)))
+            dph = dot(vall[1, :, hcols(h)], g, ((1,), (0,)))
             dsh = (hp[d, h] * (dph - stat[1, 2 * d, h : h + 1, :])).astype(BF16)
             own[1, :, hcols(h)] += dot(dsh, qall[2 * d, :, hcols(h)], ((1,), (0,)))
     dv_ref[...] = own[0].astype(BF16)
     dk_ref[...] = (own[1] * scale).astype(BF16)
-    text_third(1)
     text_last(0, tvg_ref)
     text_last(1, tkg_ref)
 
@@ -556,7 +550,8 @@
             pltpu.VMEM((heads, HD, total), BF16),
             pltpu.VMEM((heads, total, frame), F32),
             pltpu.VMEM((heads, total, frame), BF16),
-            pltpu.VMEM((heads, total, frame), F32),
+            pltpu.VMEM((heads, HD, total), BF16),
+            pltpu.VMEM((heads, HD, frame), F32),
             pltpu.VMEM((heads, total, frame), BF16),
             pltpu.VMEM((2, heads, frame, frame), F32),
             pltpu.VMEM((2, heads, frame, frame), BF16),

time: 63.6 us -> 61.3 us (0.964)
  the two profiles are of different devices: /device:TPU:706 before, /device:TPU:1 now
where the time goes in v4:
time: 61.3 us; the launch traced here: 61.1 us
  Pallas kernels  60.5 us (99%)
  between operations  0.64 us (1%)
    pallas_call x1, Pallas kernels, local(): pl.pallas_call(functools.partial(kernel, seqs, reps), out_shape=shapes, i...  58.7 us
    pallas_call x1, Pallas kernels, local(): pl.pallas_call(hand_over, out_shape=shapes, in_specs=[pl.BlockSpec(memory...  1.78 us

profile of v4, /device:TPU:1, one launch (start us, length us, event | category | flops | bytes accessed | tf_op | source)
XLA Modules:
  0.0 61.1 jit_solution(19132287673346520)
XLA Ops:
  0.6 58.7 %shard_map.128 = (bf16[256,256]{1,0:T(8,128)(2,1)}, bf16[256,256]{1,0:T(8,128)(2,1)}, bf16[256,256]{1,0:T(8,128)(2,1)}, bf16[8,256]{1,0:T(8,128)(2,1)}, bf16[8,256]{1,0:T(8,128)(2,1)}) custom-call(s32[3,128]{1,0:T(4,128)} %bitcast.2, s32[1,256]{1,0:T(1,128)} %bitcast.3, bf16[256,256]{1,0:T(8,128)(2,1)} %q_hbm.1, bf16[256,256]{1,0:T(8,128)(2,1)} %k_hbm.1, ...), custom_call_target="tpu_custom_call" | custom-call | tf_op jit(solution)/shard_map/pallas_call | solution.py:537
  59.4 1.8 %shard_map.129 = (bf16[256,256]{1,0:T(8,128)(2,1)}, bf16[256,256]{1,0:T(8,128)(2,1)}, bf16[256,256]{1,0:T(8,128)(2,1)}, bf16[8,256]{1,0:T(8,128)(2,1)}, bf16[8,256]{1,0:T(8,128)(2,1)}) custom-call(bf16[256,256]{1,0:T(8,128)(2,1)} %get-tuple-element.10.refs_0_, bf16[256,256]{1,0:T(8,128)(2,1)} %get-tuple-element.11.refs_1_, ...), custom_call_target="tpu_custom_call" | custom-call | tf_op jit(solution)/shard_map/pallas_call | solution.py:596

commit v5 on v4

--- a/solution.py
+++ b/solution.py
@@ -312,8 +312,10 @@
     def _():
         z_send_later(0)
 
-    for copy in hq:
-        copy.start()
+    @pl.when(z < 2)
+    def _():
+        for copy in hq:
+            copy.start()
 
     @pl.when(z == 1)
     def _():
@@ -334,6 +336,8 @@
                 xc[1 + d, c, e].start()
     @pl.when(z == 2)
     def _():
+        for copy in hq:
+            copy.start()
         probabilities()
 
     for b in range(1, 3):

time: 61.3 us -> 61.3 us (level)
  no operation moved by 1% of the time
where the time goes in v5:
time: 61.3 us; the launch traced here: 61.1 us
  Pallas kernels  60.5 us (99%)
  between operations  0.64 us (1%)
    pallas_call x1, Pallas kernels, local(): pl.pallas_call(functools.partial(kernel, seqs, reps), out_shape=shapes, i...  58.7 us
    pallas_call x1, Pallas kernels, local(): pl.pallas_call(hand_over, out_shape=shapes, in_specs=[pl.BlockSpec(memory...  1.78 us

profile of v5, /device:TPU:1, one launch (start us, length us, event | category | flops | bytes accessed | tf_op | source)
XLA Modules:
  0.0 61.1 jit_solution(17368266108453511704)
XLA Ops:
  0.6 58.7 %shard_map.128 = (bf16[256,256]{1,0:T(8,128)(2,1)}, bf16[256,256]{1,0:T(8,128)(2,1)}, bf16[256,256]{1,0:T(8,128)(2,1)}, bf16[8,256]{1,0:T(8,128)(2,1)}, bf16[8,256]{1,0:T(8,128)(2,1)}) custom-call(s32[3,128]{1,0:T(4,128)} %bitcast.2, s32[1,256]{1,0:T(1,128)} %bitcast.3, bf16[256,256]{1,0:T(8,128)(2,1)} %q_hbm.1, bf16[256,256]{1,0:T(8,128)(2,1)} %k_hbm.1, ...), custom_call_target="tpu_custom_call" | custom-call | tf_op jit(solution)/shard_map/pallas_call | solution.py:541
  59.4 1.8 %shard_map.129 = (bf16[256,256]{1,0:T(8,128)(2,1)}, bf16[256,256]{1,0:T(8,128)(2,1)}, bf16[256,256]{1,0:T(8,128)(2,1)}, bf16[8,256]{1,0:T(8,128)(2,1)}, bf16[8,256]{1,0:T(8,128)(2,1)}) custom-call(bf16[256,256]{1,0:T(8,128)(2,1)} %get-tuple-element.10.refs_0_, bf16[256,256]{1,0:T(8,128)(2,1)} %get-tuple-element.11.refs_1_, ...), custom_call_target="tpu_custom_call" | custom-call | tf_op jit(solution)/shard_map/pallas_call | solution.py:600

commit v6 on v4

--- a/solution.py
+++ b/solution.py
@@ -341,14 +341,20 @@
     for c in range(halves):
         for b in range(1, 3):
             add_block(c, 0, b)
-    loads[5].wait()
-    loads[6].wait()
-    for d in range(2):
-        hv[d].wait_recv()
-    for h in range(heads):
-        for j in range(4):
-            vt[h, :, j * frame : (j + 1) * frame] = vall[j, :, hcols(h)].T
-        att[h] = dot(vt[h], pt[h], ((1,), (0,)))
+    def attend():
+        loads[5].wait()
+        loads[6].wait()
+        for d in range(2):
+            hv[d].wait_recv()
+        for h in range(heads):
+            for j in range(4):
+                vt[h, :, j * frame : (j + 1) * frame] = vall[j, :, hcols(h)].T
+            att[h] = dot(vt[h], pt[h], ((1,), (0,)))
+
+    @pl.when(z < 2)
+    def _():
+        attend()
+
     for b in range(1, 3):
         for d in range(2):
             xc[b, 1 - d, d].wait_recv()
@@ -430,6 +436,19 @@
             total = total + trecv3[n, d - 1]
         out[...] = total.astype(BF16)
 
+    def dscore(j):
+        for h in range(heads):
+            for t in range(halves):
+                r = j * frame + t * TILE
+                part = dot(vall[j, rows(t), hcols(h)], gall[1, hrows(h), :], ((1,), (0,)))
+                ds[h, r : r + TILE, :] = (st[h, r : r + TILE, :] * (part - delta[h])).astype(BF16)
+
+    text_first(0, value_part)
+
+    @pl.when(z == 2)
+    def _():
+        attend()
+
     delta = []
     for h in range(heads):
         delta.append(jnp.sum(gall[1, hrows(h), :].astype(F32) * att[h], axis=0, keepdims=True))
@@ -437,14 +456,6 @@
     for copy in hd:
         copy.start()
 
-    def dscore(j):
-        for h in range(heads):
-            for t in range(halves):
-                r = j * frame + t * TILE
-                part = dot(vall[j, rows(t), hcols(h)], gall[1, hrows(h), :], ((1,), (0,)))
-                ds[h, r : r + TILE, :] = (st[h, r : r + TILE, :] * (part - delta[h])).astype(BF16)
-
-    text_first(0, value_part)
     dscore(3)
     text_first(1, lambda j, h: key_part(j, h) * scale)
     text_second(0)

time: 61.3 us -> 61.3 us (level)
  no operation moved by 1% of the time
where the time goes in v6:
time: 61.3 us; the launch traced here: 61.1 us
  Pallas kernels  60.4 us (99%)
  between operations  0.64 us (1%)
    pallas_call x1, Pallas kernels, local(): pl.pallas_call(functools.partial(kernel, seqs, reps), out_shape=shapes, i...  58.7 us
    pallas_call x1, Pallas kernels, local(): pl.pallas_call(hand_over, out_shape=shapes, in_specs=[pl.BlockSpec(memory...  1.78 us

profile of v6, /device:TPU:1, one launch (start us, length us, event | category | flops | bytes accessed | tf_op | source)
XLA Modules:
  0.0 61.1 jit_solution(84653291051582487)
XLA Ops:
  0.6 58.7 %shard_map.128 = (bf16[256,256]{1,0:T(8,128)(2,1)}, bf16[256,256]{1,0:T(8,128)(2,1)}, bf16[256,256]{1,0:T(8,128)(2,1)}, bf16[8,256]{1,0:T(8,128)(2,1)}, bf16[8,256]{1,0:T(8,128)(2,1)}) custom-call(s32[3,128]{1,0:T(4,128)} %bitcast.2, s32[1,256]{1,0:T(1,128)} %bitcast.3, bf16[256,256]{1,0:T(8,128)(2,1)} %q_hbm.1, bf16[256,256]{1,0:T(8,128)(2,1)} %k_hbm.1, ...), custom_call_target="tpu_custom_call" | custom-call | tf_op jit(solution)/shard_map/pallas_call | solution.py:548
  59.3 1.8 %shard_map.129 = (bf16[256,256]{1,0:T(8,128)(2,1)}, bf16[256,256]{1,0:T(8,128)(2,1)}, bf16[256,256]{1,0:T(8,128)(2,1)}, bf16[8,256]{1,0:T(8,128)(2,1)}, bf16[8,256]{1,0:T(8,128)(2,1)}) custom-call(bf16[256,256]{1,0:T(8,128)(2,1)} %get-tuple-element.10.refs_0_, bf16[256,256]{1,0:T(8,128)(2,1)} %get-tuple-element.11.refs_1_, ...), custom_call_target="tpu_custom_call" | custom-call | tf_op jit(solution)/shard_map/pallas_call | solution.py:607
